TPU v7x, 128 devices: a whole 4x4x4 slice. The times are simulated.
128 devices in a mesh: tok: 8 (over z, core), exp: 16 (over y, x).
Axes of the slice: x: 4, y: 4, z: 4, core: 2. Of those that a mesh axis runs over, the one named last changes fastest.
Arguments:
- x_rows: bfloat16 [3072, 4096], P(('tok', 'exp')), may hold values from -6 to 6
- routes: int32 [3072, 8], P(('tok', 'exp')), may hold values from 0 to 31, all different within a row; in each aligned block of 24 rows (0 to 23, 24 to 47, ...) at most 7 rows name the same one
- base_weight: bfloat16 [32, 1536, 4096], P('exp', 'tok'), may hold values from -6 to 6
- keep_mask: int32 [32, 24, 64], P('exp', 'tok'), may hold values 0 or 1
- dual_start: float32 [32, 1536, 4096], P('exp', 'tok'), may hold values from -4 to 4
Outputs:
- weight: float32 [32, 1536, 4096], P('exp', 'tok')
- dual: float32 [32, 1536, 4096], P('exp', 'tok')
Inputs may be any that keep to these rules, and one draw needn't show every extreme that they name: `routes`: each row names 8 different experts; among the rows of one device no expert is named more than 7 times, a bound that some block reaches; every expert is named by at least one token.
All inputs are finite; a program needn't handle non-finite values. No bound on the sum of `keep_mask` on one device may be relied on, other than what follows from the above.
Results may differ from a plain program's by a relative error of at most 0.0027.
Values may be sent and summed in bfloat16 or wider, within the bound.
A program may use at most 128 MiB of HBM per device.

v0:
```python
import jax
import jax.numpy as jnp
from jax import lax
from jax.sharding import PartitionSpec as P

EXPERTS = 32
BLOCK = 64
ITERS = 2
MOST = 7


step_rate = 0.2
penalty = 1.0


def expert_hits(routes):
    labels = jnp.arange(EXPERTS, dtype=jnp.int32)
    return jnp.any(routes[:, :, None] == labels[None, None, :], axis=1).astype(jnp.int32)


def bucket_rows(rows, routes, slots, n_exp, local_count):
    hits = expert_hits(routes)
    rank = jnp.cumsum(hits, axis=0) - hits
    slot_ids = jnp.arange(slots, dtype=jnp.int32)
    taken = (hits[:, :, None] == 1) & (rank[:, :, None] == slot_ids[None, None, :])
    taken = taken.astype(jnp.bfloat16).reshape(rows.shape[0], n_exp, local_count, slots)
    packed = jnp.einsum("rjls,rd->ljsd", taken, rows, preferred_element_type=jnp.float32)
    filled = jnp.sum(taken.astype(jnp.float32), axis=0).transpose(1, 0, 2)
    return (packed.astype(jnp.bfloat16), filled.astype(jnp.bfloat16))


def on_device(x_rows, routes, base_weight, keep_mask, dual_start):
    local_count = base_weight.shape[0]
    n_exp = lax.axis_size("exp")
    n_tok = lax.axis_size("tok")
    width = x_rows.shape[1]
    group_rows, group_routes = (
        lax.all_gather(x_rows, "tok", axis=0, tiled=True),
        lax.all_gather(routes, "tok", axis=0, tiled=True),
    )
    packed, filled = bucket_rows(group_rows, group_routes, n_tok * MOST, n_exp, local_count)
    arrived, flags = (
        lax.all_to_all(packed, "exp", split_axis=1, concat_axis=1, tiled=True),
        lax.all_to_all(filled, "exp", split_axis=1, concat_axis=1, tiled=True),
    )
    counts = jnp.sum(flags.astype(jnp.float32).reshape(local_count, -1), axis=1)
    expert_rows = arrived.reshape(local_count, -1, width)
    mask = jnp.repeat(jnp.repeat(keep_mask.astype(jnp.float32), BLOCK, 1), BLOCK, 2)
    base32 = base_weight.astype(jnp.float32)
    weight = mask * base32
    zed = weight
    dual = dual_start
    for step in range(ITERS):
        delta = (weight - base32).astype(jnp.bfloat16)
        resid = jnp.einsum(
            "lnd,lcd->lnc", expert_rows, delta, preferred_element_type=jnp.float32
        ).astype(jnp.bfloat16)
        grad = (
            jnp.einsum("lnc,lnd->lcd", resid, expert_rows, preferred_element_type=jnp.float32)
            / counts[:, None, None]
        )
        weight = weight - step_rate * (grad + penalty * (weight - zed + dual))
        zed = mask * (weight + dual)
        dual = dual + weight - zed
    return (weight, dual)


def solution(mesh):
    return jax.shard_map(
        on_device,
        mesh=mesh,
        in_specs=(
            P(("tok", "exp"), None),
            P(("tok", "exp"), None),
            P("exp", "tok", None),
            P("exp", "tok", None),
            P("exp", "tok", None),
        ),
        out_specs=(P("exp", "tok", None), P("exp", "tok", None)),
        check_vma=False,
    )
```

profile of v0, /device:TPU:1, one launch (start us, length us, event | category | flops | bytes accessed | tf_op | source)
XLA Modules:
  0.0 344.4 jit_solution(4313920032585613307)
XLA Ops:
  7.2 0.0 all-gather.3.cloned.1.call-start
  7.2 0.7 all-gather.3.cloned.1.call-update
  7.9 15.6 %all-gather = s32[8,24,8]{1,2,0:T(8,128)S(1)} all-gather(s32[1,24,8]{1,2,0:T(8,128)} %bitcast.44), channel_id=1, replica_groups=mesh['tok'=8,'exp'=16] {'tok'}, dimensions={0}, use_global_device_ids=true | all-gather | bytes 6912 | tf_op jit(solution)/shard_map/all_gather | solution.py:39
  23.5 0.1 reshape.52
  23.6 0.6 reduce-window.6
  24.2 0.2 slice_reduce_fusion
  24.4 0.1 bitcast_bitcast_fusion
  24.6 1.0 fusion.16
  25.6 6.8 %all-to-all-start.1 = ((bf16[2,16,56]{2,0,1:T(2,128)(2,1)}), bf16[2,16,56]{2,0,1:T(2,128)(2,1)S(1)}, u32[]{:S(2)}, u32[]{:S(2)}) async-start(bf16[2,16,56]{2,0,1:T(2,128)(2,1)} %bitcast.9), calls=%async_computation.1 | async-start | bytes 16384 | tf_op jit(solution)/shard_map/all_to_all | solution.py:44
  32.4 5.5 %all-gather.3.cloned.1.call-done = bf16[192,4096]{1,0:T(8,128)(2,1)} async-done(((bf16[24,4096]{1,0:T(8,128)(2,1)}), bf16[192,4096]{1,0:T(8,128)(2,1)}) %all-gather.3.cloned.1.call-update) | async-done | bytes 1572880 | tf_op jit(solution)/shard_map/all_gather | solution.py:38
  37.9 8.7 %convert_bitcast_fusion = bf16[2,16,56,4096]{3,2,0,1:T(8,128)(2,1)} fusion(bf16[192,4096]{1,0:T(8,128)(2,1)} %all-gather.3.cloned.1.call-done, s32[192,16,2]{0,2,1:T(2,128)S(1)} %eq.50, pred[192,16,2]{0,2,1:T(4,128)(4,1)S(1)} %eq.49), kind=kOutput, calls=%fused_computation | convolution fusion | flops 2826600448 | bytes 16283648 | tf_op jit(solution)/shard_map/rjls,rd->ljsd/dot_general | solution.py:27
  46.6 0.0 copy-start.1
  46.6 0.0 all-to-all-done.1
  46.6 6.7 %all-to-all-start = ((bf16[2,16,56,4096]{3,2,0,1:T(8,128)(2,1)}), bf16[2,16,56,4096]{3,2,0,1:T(8,128)(2,1)}, u32[]{:S(2)}, u32[]{:S(2)}) async-start(bf16[2,16,56,4096]{3,2,0,1:T(8,128)(2,1)} %convert_bitcast_fusion), calls=%async_computation | async-start | bytes 29360128 | tf_op jit(solution)/shard_map/all_to_all | solution.py:43
  53.3 0.0 copy-done.1
  53.4 0.1 copy.57
  53.5 4.0 %broadcast_in_dim.5 = f32[2,192,64,64]{1,3,2,0:T(8,128)} broadcast(f32[2,192,64]{1,2,0:T(8,128)S(1)} %copy.57), dimensions={0,1,2} | broadcast | bytes 6389760 | tf_op jit(solution)/shard_map/broadcast_in_dim | solution.py:48
  57.5 8.2 %copy.58 = f32[2,192,4096]{2,1,0:T(8,128)} copy(f32[2,192,4096]{1,2,0:T(8,128)} %bitcast.37) | data formatting | bytes 12582912 | tf_op jit(solution)/shard_map/reshape | solution.py:48
  65.7 0.1 convert_reduce_fusion
  65.8 206.9 %all-to-all-done = bf16[2,16,56,4096]{3,2,0,1:T(8,128)(2,1)} async-done(((bf16[2,16,56,4096]{3,2,0,1:T(8,128)(2,1)}), bf16[2,16,56,4096]{3,2,0,1:T(8,128)(2,1)}, u32[]{:S(2)}, u32[]{:S(2)}) %all-to-all-start) | async-done | bytes 14680096 | tf_op jit(solution)/shard_map/all_to_all | solution.py:43
  272.7 0.0 copy-start
  272.7 0.0 slice-start
  272.7 15.2 %copy.62 = bf16[2,16,56,4096]{3,2,1,0:T(8,128)(2,1)} copy(bf16[2,16,56,4096]{3,2,0,1:T(8,128)(2,1)} %all-to-all-done) | data formatting | bytes 29360128 | tf_op jit(solution)/shard_map/all_to_all | solution.py:43
  287.9 0.0 copy-done
  287.9 0.0 slice-start.1
  287.9 9.8 %fusion.10 = bf16[2,896,192]{1,2,0:T(8,128)(2,1)} fusion(bf16[2,896,4096]{2,1,0:T(8,128)(2,1)} %bitcast.38, bf16[2,192,4096]{2,1,0:T(8,128)(2,1)} %param.7, f32[2,192,4096]{2,1,0:T(8,128)S(1)} %copy-done), kind=kOutput, calls=%fused_computation.16 | convolution fusion | flops 2825207808 | bytes 24805376 | tf_op jit(solution)/shard_map/lnd,lcd->lnc/dot_general | solution.py:55
  297.7 0.0 slice-done
  297.7 0.0 slice-done.1
  297.7 13.9 %multiply_subtract_fusion.2 = f32[2,192,4096]{2,1,0:T(8,128)} fusion(f32[2,192,4096]{2,1,0:T(8,128)S(1)} %bitcast.46, f32[2,192,4096]{2,1,0:T(8,128)S(1)} %copy-done, bf16[2,192,4096]{2,1,0:T(8,128)(2,1)} %param.7, bf16[2,896,192]{1,2,0:T(8,128)(2,1)} %fusion.10, bf16[2,896,4096]{2,1,0:T(8,128)(2,1)} %bitcast.39, f32[2]{0:T(128)S(1)} %convert_reduce_fusion), kind=kOutput, calls=%fused_computation.8 | convolution fusion | flops 2831155200 | bytes 37388296 | tf_op jit(solution)/shard_map/lnc,lnd->lcd/dot_general | solution.py:59
  311.6 11.3 %fusion.13 = bf16[2,896,192]{1,2,0:T(8,128)(2,1)} fusion(bf16[2,896,4096]{2,1,0:T(8,128)(2,1)} %bitcast.40, f32[2,192,4096]{2,1,0:T(8,128)} %multiply_subtract_fusion.2, bf16[2,192,4096]{2,1,0:T(8,128)(2,1)} %param.7), kind=kOutput, calls=%fused_computation.17 | convolution fusion | flops 2823634944 | bytes 24805376 | tf_op jit(solution)/shard_map/lnd,lcd->lnc/dot_general | solution.py:55
  322.9 14.6 %multiply_subtract_fusion = (f32[2,192,4096]{2,1,0:T(8,128)}, f32[2,192,4096]{2,1,0:T(8,128)}) fusion(f32[2,192,4096]{2,1,0:T(8,128)S(1)} %copy-done, f32[2,192,4096]{2,1,0:T(8,128)} %multiply_subtract_fusion.2, f32[2,192,4096]{2,1,0:T(8,128)} %param.9, f32[2]{0:T(128)S(1)} %convert_reduce_fusion, bf16[2,896,192]{1,2,0:T(8,128)(2,1)} %fusion.13, ...), kind=kOutput, calls=%fused_computation.1 | convolution fusion | flops 2837446656 | bytes 46825480 | tf_op jit(solution)/shard_map/lnc,lnd->lcd/dot_general | solution.py:59
  (13 shorter events, 0.2 us)
Async XLA Ops:
  7.2 30.7 %all-gather.3.cloned.1.call-start = ((), (), s32[]{:S(2)}) async-start(), calls=%async_computation.2 | async-start | bytes 1769472 | tf_op jit(solution)/shard_map/all_gather | solution.py:38
  25.6 20.9 %all-to-all-start.1 = ((bf16[2,16,56]{2,0,1:T(2,128)(2,1)}), bf16[2,16,56]{2,0,1:T(2,128)(2,1)S(1)}, u32[]{:S(2)}, u32[]{:S(2)}) async-start(bf16[2,16,56]{2,0,1:T(2,128)(2,1)} %bitcast.9), calls=%async_computation.1 | async-start | bytes 16384 | tf_op jit(solution)/shard_map/all_to_all | solution.py:44
  46.6 6.7 %copy-start.1 = (s32[2,3,64]{2,0,1:T(2,128)S(1)}, s32[2,3,64]{2,0,1:T(2,128)}, u32[]{:S(2)}) copy-start(s32[2,3,64]{2,0,1:T(2,128)} %param.8) | copy-start | bytes 4612
  46.6 226.1 %all-to-all-start = ((bf16[2,16,56,4096]{3,2,0,1:T(8,128)(2,1)}), bf16[2,16,56,4096]{3,2,0,1:T(8,128)(2,1)}, u32[]{:S(2)}, u32[]{:S(2)}) async-start(bf16[2,16,56,4096]{3,2,0,1:T(8,128)(2,1)} %convert_bitcast_fusion), calls=%async_computation | async-start | bytes 29360128 | tf_op jit(solution)/shard_map/all_to_all | solution.py:43
  272.7 15.2 %copy-start = (f32[2,192,4096]{2,1,0:T(8,128)S(1)}, f32[2,192,4096]{2,1,0:T(8,128)}, u32[]{:S(2)}) copy-start(f32[2,192,4096]{2,1,0:T(8,128)} %copy.58) | copy-start | bytes 18874372
  272.7 25.0 %slice-start = ((s8[6291456]{0:T(1024)(128)(4,1)}), s8[4194304]{0:T(1024)(128)(4,1)S(1)}, s32[]{:S(2)}) async-start(s8[6291456]{0:T(1024)(128)(4,1)} %bitcast.45), calls=%async_computation.3 | async-start | bytes 8388608
  287.9 9.8 %slice-start.1 = ((s8[6291456]{0:T(1024)(128)(4,1)}), s8[2097152]{0:T(1024)(128)(4,1)S(1)}, s32[]{:S(2)}) async-start(s8[6291456]{0:T(1024)(128)(4,1)} %bitcast.45), calls=%async_computation.4 | async-start | bytes 4194304
Sparse Core Ops, SparseCore 0:
  9.7 28.2 all-gather.2
where the time goes:
time: 345 us; the launch traced here: 344 us
  waiting for transfers between devices  213 us (62%)
  matrix products  58.3 us (17%)
  local copies, waits for them, and re-layouts  27.8 us (8%)
  blocking collectives  15.6 us (5%)
  between operations  14.1 us (4%)
  starting transfers between devices  13.5 us (4%)
    all_to_all x1, waiting for transfers between devices, on_device(): lax.all_to_all(packed, 'exp', split_axis=1, concat_axis=1, tiled=True)  207 us
    dot_general x2, matrix products, on_device(): jnp.einsum('lnc,lnd->lcd', resid, expert_rows, preferred_element_type=jnp...  28.5 us
    dot_general x2, matrix products, on_device(): jnp.einsum('lnd,lcd->lnc', expert_rows, delta, preferred_element_type=jnp...  21.2 us
    all_gather x1, blocking collectives, on_device(): lax.all_gather(routes, 'tok', axis=0, tiled=True)  15.6 us
    all_to_all x1, local copies, waits for them, and re-layouts, on_device(): lax.all_to_all(packed, 'exp', split_axis=1, concat_axis=1, tiled=True)  15.2 us
    dot_general x1, matrix products, bucket_rows(): jnp.einsum('rjls,rd->ljsd', taken, rows, preferred_element_type=jnp.float32)  8.67 us
    reshape x1, local copies, waits for them, and re-layouts, on_device(): jnp.repeat(jnp.repeat(keep_mask.astype(jnp.float32), BLOCK, 1), BLOCK, 2)  8.25 us
  transfers between devices with their start and end apart: 3, of which 2 were waited for; matrix products, arithmetic and copies ran while one was open for 7% of the time, Pallas kernels for 0%

commit v1 on v0

v1 whole, which is shorter than its diff:
```python
import functools
import jax
import jax.numpy as jnp
from jax import lax
from jax.experimental import pallas as pl
from jax.experimental.pallas import tpu as pltpu

SLOTS = 896
HL = 192
D = 4096
CW = 512
NC = D // CW
BLOCK = 64
step_rate = 0.2
penalty = 1.0


def dot(a, b, ca, cb):
    return lax.dot_general(a, b, (((ca,), (cb,)), ((), ())), preferred_element_type=jnp.float32)


def tail_kernel(xc_hbm, r1_ref, base_hbm, dual_hbm, rm_ref, inv_ref, w_hbm, d_hbm,
                xc, base, dual, w1, r2, r2b, ow, od, sin, sout):
    def fetch(j):
        cols = pl.ds(j * CW, CW)
        return [
            pltpu.make_async_copy(xc_hbm.at[:, :, cols], xc.at[:, :, cols], sin.at[0, j]),
            pltpu.make_async_copy(base_hbm.at[:, :, cols], base.at[:, :, cols], sin.at[1, j]),
            pltpu.make_async_copy(dual_hbm.at[:, :, cols], dual.at[:, :, cols], sin.at[2, j]),
        ]
    for j in range(NC):
        for c in fetch(j):
            c.start()

    def mask_of(e, j):
        kb = lax.broadcasted_iota(jnp.int32, (BLOCK, CW), 0)
        cb = lax.broadcasted_iota(jnp.int32, (BLOCK, CW), 1) // BLOCK + j * (CW // BLOCK)
        sel = (kb == cb).astype(jnp.bfloat16)
        return dot(rm_ref[e], sel, 1, 0)

    def pass1(j, _):
        off = pl.multiple_of(j * CW, CW)
        cols = pl.ds(off, CW)
        for i, (h, v) in enumerate(((xc_hbm, xc), (base_hbm, base), (dual_hbm, dual))):
            pltpu.make_async_copy(h.at[:, :, cols], v.at[:, :, cols], sin.at[i, j]).wait()
        for e in range(2):
            x = xc[e, :, cols]
            g = dot(r1_ref[e], x, 1, 0) * inv_ref[e, 0:1, 0:1]
            m = mask_of(e, j)
            b = base[e, :, cols].astype(jnp.float32)
            w = m * b - step_rate * (g + penalty * dual[e, :, cols])
            w1[e, :, cols] = w
            dl = (w - b).astype(jnp.bfloat16)
            r = dot(dl, x, 1, 1)
            @pl.when(j == 0)
            def _():
                r2[e] = r
            @pl.when(j > 0)
            def _():
                r2[e] += r
        return 0
    lax.fori_loop(0, NC, pass1, 0)
    for e in range(2):
        r2b[e] = r2[e].astype(jnp.bfloat16)

    def outs(slot, off):
        cols = pl.ds(off, CW)
        return [
            pltpu.make_async_copy(ow.at[slot], w_hbm.at[:, :, cols], sout.at[0, slot]),
            pltpu.make_async_copy(od.at[slot], d_hbm.at[:, :, cols], sout.at[1, slot]),
        ]

    def pass2(j, _):
        off = pl.multiple_of(j * CW, CW)
        cols = pl.ds(off, CW)
        slot = j % 2
        @pl.when(j >= 2)
        def _():
            for c in outs(slot, off):
                c.wait()
        for e in range(2):
            g = dot(r2b[e], xc[e, :, cols], 1, 0) * inv_ref[e, 0:1, 0:1]
            m = mask_of(e, j)
            d0 = dual[e, :, cols]
            w = w1[e, :, cols]
            z = m * (w + d0)
            d1 = d0 + w - z
            w2 = w - step_rate * (g + penalty * (w - z + d1))
            z2 = m * (w2 + d1)
            ow[slot, e] = w2
            od[slot, e] = d1 + w2 - z2
        for c in outs(slot, off):
            c.start()
        return 0
    lax.fori_loop(0, NC, pass2, 0)
    for slot in range(2):
        for c in outs(slot, 0):
            c.wait()


def tail(xc, r1t, base, dual, rowmask, inv):
    any_ = pl.BlockSpec(memory_space=pl.ANY)
    vm = pl.BlockSpec(memory_space=pltpu.VMEM)
    out = jax.ShapeDtypeStruct((2, HL, D), jnp.float32)
    return pl.pallas_call(
        tail_kernel,
        out_shape=(out, out),
        in_specs=[any_, vm, any_, any_, vm, vm],
        out_specs=(any_, any_),
        scratch_shapes=[
            pltpu.VMEM((2, SLOTS, D), jnp.bfloat16),
            pltpu.VMEM((2, HL, D), jnp.bfloat16),
            pltpu.VMEM((2, HL, D), jnp.float32),
            pltpu.VMEM((2, HL, D), jnp.float32),
            pltpu.VMEM((2, HL, SLOTS), jnp.float32),
            pltpu.VMEM((2, HL, SLOTS), jnp.bfloat16),
            pltpu.VMEM((2, 2, HL, CW), jnp.float32),
            pltpu.VMEM((2, 2, HL, CW), jnp.float32),
            pltpu.SemaphoreType.DMA((3, NC)),
            pltpu.SemaphoreType.DMA((2, 2)),
        ],
        compiler_params=pltpu.CompilerParams(vmem_limit_bytes=60 * 1024 * 1024),
        name="tail",
    )(xc, r1t, base, dual, rowmask, inv)


def front(x_rows, routes, base_weight, keep_mask):
    rows = lax.all_gather(x_rows, ("tok", "exp"), axis=0, tiled=True)
    rts = lax.all_gather(routes, ("tok", "exp"), axis=0, tiled=True)
    e0 = 2 * lax.axis_index("exp")
    hits = jnp.stack([jnp.any(rts == e0 + i, axis=1) for i in range(2)]).astype(jnp.bfloat16)
    counts = jnp.sum(hits.astype(jnp.float32), axis=1)
    h = hits.reshape(2, 8, 384)
    up = (jnp.arange(384)[:, None] < jnp.arange(384)[None, :]).astype(jnp.bfloat16)
    rank = jnp.einsum("egr,rs->egs", h, up, preferred_element_type=jnp.float32)
    slot = jnp.where(h > 0, rank, -1.0)
    p = (slot[:, :, None, :] == jnp.arange(112, dtype=jnp.float32)[None, None, :, None]).astype(jnp.bfloat16)
    xc = jnp.einsum("egsr,grd->egsd", p, rows.reshape(8, 384, D), preferred_element_type=jnp.float32)
    xc = xc.astype(jnp.bfloat16).reshape(2, SLOTS, D)
    mask = jnp.repeat(jnp.repeat(keep_mask.astype(jnp.float32), BLOCK, 1), BLOCK, 2)
    delta = ((mask - 1.0) * base_weight.astype(jnp.float32)).astype(jnp.bfloat16)
    r1t = jnp.einsum("lcd,lnd->lcn", delta, xc, preferred_element_type=jnp.float32).astype(jnp.bfloat16)
    return xc, r1t, counts


def on_device(x_rows, routes, base_weight, keep_mask, dual_start):
    xc, r1t, counts = front(x_rows, routes, base_weight, keep_mask)
    rowmask = jnp.repeat(keep_mask, BLOCK, 1).astype(jnp.bfloat16)
    inv = jnp.broadcast_to((1.0 / counts)[:, None, None], (2, 8, 128))
    return tail(xc, r1t, base_weight, dual_start, rowmask, inv)


def solution(mesh):
    from jax.sharding import PartitionSpec as P
    return jax.shard_map(
        on_device,
        mesh=mesh,
        in_specs=(
            P(("tok", "exp"), None),
            P(("tok", "exp"), None),
            P("exp", "tok", None),
            P("exp", "tok", None),
            P("exp", "tok", None),
        ),
        out_specs=(P("exp", "tok", None), P("exp", "tok", None)),
        check_vma=False,
    )
```

time: 345 us -> 189 us (0.55)
  waiting for transfers between devices: 213 us -> 24.1 us
  blocking collectives: 15.6 us -> 61.7 us
  matrix products: 58.3 us -> 30.7 us
  Pallas kernels: 0 us -> 26.4 us
  starting transfers between devices: 13.5 us -> 0.04 us
    all_to_all x2 -> x0, waiting for transfers between devices: 207 us -> none  [the longest x1 207 us: on_device(): lax.all_to_all(packed, 'exp', split_axis=1, concat_axis=1, tiled=True)]
    all_gather x1, blocking collectives: 15.6 us -> 61.7 us  [front(): rts = lax.all_gather(routes, ('tok', 'exp'), axis=0, tiled=True)]
    dot_general x5 -> x3, matrix products: 58.3 us -> 30.7 us  [the longest x1 19.6 us: front(): jnp.einsum('egsr,grd->egsd', p, rows.reshape(8, 384, D), preferred_elemen...]
    pallas_call x0 -> x1, Pallas kernels: none -> 26.4 us  [tail(): pl.pallas_call(tail_kernel, out_shape=(out, out), in_specs=[any_, vm, any...]
    all_gather x1, waiting for transfers between devices: 5.5 us -> 23.4 us  [front(): rows = lax.all_gather(x_rows, ('tok', 'exp'), axis=0, tiled=True)]
    all_to_all x1 -> x0, local copies, waits for them, and re-layouts: 15.2 us -> none  [on_device(): lax.all_to_all(packed, 'exp', split_axis=1, concat_axis=1, tiled=True)]
    convert_element_type x1 -> x2, local copies, waits for them, and re-layouts: 0.01 us -> 14.9 us  [the longest x1 14.9 us: front(): xc = xc.astype(jnp.bfloat16).reshape(2, SLOTS, D)]
    all_to_all x2 -> x0, starting transfers between devices: 13.5 us -> none  [the longest x1 6.75 us: on_device(): lax.all_to_all(filled, 'exp', split_axis=1, concat_axis=1, tiled=True)]
  transfers between devices with their start and end apart: 3 -> 1, of which waited for: 2 -> 1; matrix products, arithmetic and copies ran while one was open for 7% -> 8% of each run, Pallas kernels for 0% -> 0%
where the time goes in v1:
time: 189 us; the launch traced here: 188 us
  blocking collectives  61.7 us (33%)
  matrix products  30.7 us (16%)
  local copies, waits for them, and re-layouts  29.1 us (15%)
  Pallas kernels  26.4 us (14%)
  waiting for transfers between devices  24.1 us (13%)
  between operations  14.1 us (7%)
  other arithmetic  1.9 us (1%)
    all_gather x1, blocking collectives, front(): rts = lax.all_gather(routes, ('tok', 'exp'), axis=0, tiled=True)  61.7 us
    pallas_call x1, Pallas kernels, tail(): pl.pallas_call(tail_kernel, out_shape=(out, out), in_specs=[any_, vm, any...  26.4 us
    all_gather x1, waiting for transfers between devices, front(): rows = lax.all_gather(x_rows, ('tok', 'exp'), axis=0, tiled=True)  23.4 us
    dot_general x1, matrix products, front(): jnp.einsum('egsr,grd->egsd', p, rows.reshape(8, 384, D), preferred_elemen...  19.6 us
    convert_element_type x1, local copies, waits for them, and re-layouts, front(): xc = xc.astype(jnp.bfloat16).reshape(2, SLOTS, D)  14.9 us
    dot_general x1, matrix products, front(): jnp.einsum('lcd,lnd->lcn', delta, xc, preferred_element_type=jnp.float32)  11 us
    sub x3, local copies, waits for them, and re-layouts, front(): mask - 1.0  8.41 us
    broadcast_in_dim x1, local copies, waits for them, and re-layouts, front(): jnp.repeat(jnp.repeat(keep_mask.astype(jnp.float32), BLOCK, 1), BLOCK, 2)  3.97 us
  transfers between devices with their start and end apart: 1, of which 1 were waited for; matrix products, arithmetic and copies ran while one was open for 8% of the time, Pallas kernels for 0%

profile of v1, /device:TPU:1, one launch (start us, length us, event | category | flops | bytes accessed | tf_op | source)
XLA Modules:
  0.0 188.0 jit_solution(6519917828813212423)
XLA Ops:
  7.2 0.0 all-gather.3.cloned.1.call-start
  7.2 0.7 all-gather.3.cloned.1.call-update
  7.9 61.7 %all-gather = s32[128,24,8]{1,2,0:T(8,128)S(1)} all-gather(s32[1,24,8]{1,2,0:T(8,128)} %bitcast.24), channel_id=1, replica_groups=mesh['tok'=8,'exp'=16] {'tok','exp'}, dimensions={0}, use_global_device_ids=true | all-gather | bytes 99072 | tf_op jit(solution)/shard_map/all_gather | solution.py:129
  69.6 0.4 compare_reduce_fusion
  69.9 0.1 stack.15
  70.0 0.1 stack.18
  70.1 0.1 stack.16
  70.3 0.1 stack.19
  70.4 0.1 convolution_select_fusion
  70.6 0.7 convert_element_type.41
  71.3 0.7 convert_add_fusion
  72.0 0.1 copy.33
  72.1 4.0 %broadcast_in_dim.25 = f32[2,192,64,64]{1,3,2,0:T(8,128)} broadcast(f32[2,192,64]{1,2,0:T(8,128)S(1)} %copy.33), dimensions={0,1,2} | broadcast | bytes 6389760 | tf_op jit(solution)/shard_map/broadcast_in_dim | solution.py:140
  76.1 8.3 %copy.34 = f32[2,192,4096]{2,1,0:T(8,128)} copy(f32[2,192,4096]{1,2,0:T(8,128)} %bitcast.20) | data formatting | bytes 12582912 | tf_op jit(solution)/shard_map/sub | solution.py:141
  84.4 0.1 convert_reduce_fusion
  84.5 23.4 %all-gather.3.cloned.1.call-done = bf16[3072,4096]{1,0:T(8,128)(2,1)} async-done(((bf16[24,4096]{1,0:T(8,128)(2,1)}), bf16[3072,4096]{1,0:T(8,128)(2,1)}) %all-gather.3.cloned.1.call-update) | async-done | bytes 25165840 | tf_op jit(solution)/shard_map/all_gather | solution.py:128
  108.0 19.6 %convert_bitcast_fusion = bf16[2,8,112,4096]{3,2,0,1:T(8,128)(2,1)} fusion(bf16[8,384,4096,1]{2,1,3,0:T(8,128)(2,1)} %bitcast.21, f32[2,8,384]{2,0,1:T(2,128)S(1)} %copy.30), kind=kOutput, calls=%fused_computation | convolution fusion | flops 5645172736 | bytes 39870464 | tf_op jit(solution)/shard_map/egsr,grd->egsd/dot_general | solution.py:138
  127.5 0.0 copy-start
  127.5 0.0 copy-start.1
  127.5 14.9 %copy.31 = bf16[2,8,112,4096]{3,2,1,0:T(8,128)(2,1)} copy(bf16[2,8,112,4096]{3,2,0,1:T(8,128)(2,1)} %convert_bitcast_fusion) | data formatting | bytes 29360128 | tf_op jit(solution)/shard_map/convert_element_type | solution.py:139
  142.4 0.0 copy-done
  142.4 0.0 copy-done.1
  142.4 11.0 %fusion.2.r1_ref = bf16[2,192,896]{2,1,0:T(8,128)(2,1)} fusion(bf16[2,896,4096]{2,1,0:T(8,128)(2,1)} %bitcast.18, f32[2,192,4096]{2,1,0:T(8,128)S(1)} %copy-done, bf16[2,192,4096]{2,1,0:T(8,128)(2,1)S(1)} %copy-done.1), kind=kOutput, calls=%fused_computation.5 | convolution fusion | flops 2823634944 | bytes 24805376 | tf_op jit(solution)/shard_map/lcd,lnd->lcn/dot_general | solution.py:142
  153.4 0.7 broadcast_in_dim.27.inv_ref
  154.1 0.6 broadcast_in_dim.26
  154.7 26.4 %tail.1 = (f32[2,192,4096]{2,1,0:T(8,128)}, f32[2,192,4096]{2,1,0:T(8,128)}) custom-call(bf16[2,896,4096]{2,1,0:T(8,128)(2,1)} %bitcast.19, bf16[2,192,896]{2,1,0:T(8,128)(2,1)} %fusion.2.r1_ref, bf16[2,192,4096]{2,1,0:T(8,128)(2,1)} %base_hbm.1, f32[2,192,4096]{2,1,0:T(8,128)} %dual_hbm.1, bf16[2,192,64]{2,1,0:T(8,128)(2,1)} %bitcast.23, ...), custom_call_target="tpu_custom_call" | custom-call | tf_op jit(solution)/shard_map/tail/pallas_call | solution.py:105
  (7 shorter events, 0.1 us)
Async XLA Ops:
  7.2 100.8 %all-gather.3.cloned.1.call-start = ((), (), s32[]{:S(2)}) async-start(), calls=%async_computation | async-start | bytes 25362432 | tf_op jit(solution)/shard_map/all_gather | solution.py:128
  127.5 14.9 %copy-start = (f32[2,192,4096]{2,1,0:T(8,128)S(1)}, f32[2,192,4096]{2,1,0:T(8,128)}, u32[]{:S(2)}) copy-start(f32[2,192,4096]{2,1,0:T(8,128)} %copy.34) | copy-start | bytes 18874372
  127.5 14.9 %copy-start.1 = (bf16[2,192,4096]{2,1,0:T(8,128)(2,1)S(1)}, bf16[2,192,4096]{2,1,0:T(8,128)(2,1)}, u32[]{:S(2)}) copy-start(bf16[2,192,4096]{2,1,0:T(8,128)(2,1)} %base_hbm.1) | copy-start | bytes 9437188
Sparse Core Ops, SparseCore 0:
  11.0 96.9 all-gather.2
